TPU v7x, 768 devices: a whole 4x8x12 slice. The times are simulated.
768 devices in a mesh: slab: 16 (over y, x_hi), chan: 48 (over z, x_lo, core).
Axes of the slice: x: 4 (x_hi: 2, x_lo: 2; x = x_hi * 2 + x_lo), y: 8, z: 12, core: 2. Of those that a mesh axis runs over, the one named last changes fastest.
Arguments:
- volume: bfloat16 [32, 96, 64, 256], P('slab', 'chan'), may hold values from -6 to 6
- weights: bfloat16 [6912, 256], P(None, 'slab'), may hold values from -0.078125 to 0.078125
Outputs:
- conv_out: bfloat16 [32, 96, 64, 256], P('slab', 'chan')
All inputs are finite; a program needn't handle non-finite values.
Results may differ from a plain program's by a relative error of at most 0.001.
Values may be sent and summed in bfloat16 or wider, within the bound.
A program may use at most 32 MiB of HBM per device.

v0:
```python
import jax
import jax.numpy as jnp
from jax import lax
from jax.sharding import PartitionSpec as P


def extended_2(block, sides, width):
    for axis, dim in sides:
        count = lax.axis_size(axis)
        forward = [(i, i + 1) for i in range(count - 1)]
        backward = [(target, source) for source, target in forward]
        low = lax.ppermute(
            lax.slice_in_dim(block, block.shape[dim] - width, None, axis=dim), axis, forward
        )
        high = lax.ppermute(lax.slice_in_dim(block, 0, width, axis=dim), axis, backward)
        block = jnp.concatenate([low, block, high], axis=dim)
    return block


def local(volume, weights):
    depth_cells, row_cells, col_cells, channels = volume.shape
    voxels = depth_cells * row_cells * col_cells
    extended = extended_2(volume, (("slab", 0), ("chan", 1)), 1)
    padded = jnp.pad(extended, ((0, 0), (0, 0), (1, 1), (0, 0)))
    gathered = lax.all_gather(weights, "slab", axis=1, tiled=True)
    out_width = gathered.shape[1]
    summed = jnp.zeros((voxels, out_width), jnp.float32)
    for depth_off in range(3):
        pieces = []
        for row_off in range(3):
            for col_off in range(3):
                shifted = padded[
                    depth_off : depth_off + depth_cells,
                    row_off : row_off + row_cells,
                    col_off : col_off + col_cells,
                    :,
                ]
                pieces.append(shifted.reshape(voxels, channels))
        columns = jnp.concatenate(pieces, axis=1)
        kernel_rows = gathered[9 * depth_off * channels : (9 * depth_off + 9) * channels, :]
        summed = summed + jnp.dot(columns, kernel_rows, preferred_element_type=jnp.float32)
    return summed.astype(jnp.bfloat16).reshape(depth_cells, row_cells, col_cells, channels)


def solution(mesh):
    placed = (P("slab", "chan", None, None), P(None, "slab"))
    return jax.shard_map(
        local, mesh=mesh, in_specs=placed, out_specs=P("slab", "chan", None, None), check_vma=False
    )
```

profile of v0, /device:TPU:1, one launch (start us, length us, event | category | flops | bytes accessed | tf_op | source)
XLA Modules:
  0.0 134.8 jit_solution(5294865338269816323)
XLA Ops:
  6.5 0.0 all-gather.2.cloned.1.call-start
  6.5 0.7 all-gather.2.cloned.1.call-update
  7.3 0.9 fusion.27
  8.1 5.5 %collective-permute-start = (bf16[1,2,64,256]{3,2,1,0:T(8,128)(2,1)S(1)}, bf16[1,2,64,256]{3,2,1,0:T(8,128)(2,1)S(1)}, u32[]{:S(2)}, u32[]{:S(2)}) collective-permute-start(bf16[1,2,64,256]{3,2,1,0:T(8,128)(2,1)S(1)} %get-tuple-element.38), channel_id=1, source_target_pairs={{0,48},{48,96},{96,144},{144,192},{192,240},{240,288},{288,336},{3... | collective-permute-start | bytes 196616 | tf_op jit(solution)/shard_map/ppermute | solution.py:12
  13.6 1.3 collective-permute-start.1
  14.9 0.0 collective-permute-done
  15.0 5.2 %collective-permute-done.1 = bf16[1,2,64,256]{3,2,1,0:T(8,128)(2,1)S(1)} collective-permute-done((bf16[1,2,64,256]{3,2,1,0:T(8,128)(2,1)S(1)}, bf16[1,2,64,256]{3,2,1,0:T(8,128)(2,1)S(1)}, u32[]{:S(2)}, u32[]{:S(2)}) %collective-permute-start.1) | collective-permute-done | bytes 65568 | tf_op jit(solution)/shard_map/ppermute | solution.py:15
  20.1 1.0 pad_maximum_fusion.3
  21.2 9.4 %collective-permute-start.3 = (bf16[4,1,64,256]{3,2,1,0:T(8,128)(2,1)S(1)}, bf16[4,1,64,256]{3,2,1,0:T(8,128)(2,1)S(1)}, u32[]{:S(2)}, u32[]{:S(2)}) collective-permute-start(bf16[4,1,64,256]{3,2,1,0:T(8,128)(2,1)S(1)} %get-tuple-element.33), channel_id=1, source_target_pairs={{1,0},{2,1},{3,2},{4,3},{5,4},{6,5},{7,6},{8,7},{9,8},{10,9},{11,1... | collective-permute-start | bytes 393224 | tf_op jit(solution)/shard_map/ppermute | solution.py:15
  30.6 1.9 %collective-permute-start.2 = (bf16[4,1,64,256]{3,2,1,0:T(8,128)(2,1)S(1)}, bf16[4,1,64,256]{3,2,1,0:T(8,128)(2,1)S(1)}, u32[]{:S(2)}, u32[]{:S(2)}) collective-permute-start(bf16[4,1,64,256]{3,2,1,0:T(8,128)(2,1)S(1)} %get-tuple-element.32), channel_id=1, source_target_pairs={{0,1},{1,2},{2,3},{3,4},{4,5},{5,6},{6,7},{7,8},{8,9},{9,10},{10,1... | collective-permute-start | bytes 393224 | tf_op jit(solution)/shard_map/ppermute | solution.py:12
  32.5 0.0 collective-permute-done.3
  32.5 1.9 %collective-permute-done.2 = bf16[4,1,64,256]{3,2,1,0:T(8,128)(2,1)S(1)} collective-permute-done((bf16[4,1,64,256]{3,2,1,0:T(8,128)(2,1)S(1)}, bf16[4,1,64,256]{3,2,1,0:T(8,128)(2,1)S(1)}, u32[]{:S(2)}, u32[]{:S(2)}) %collective-permute-start.2) | collective-permute-done | bytes 131104 | tf_op jit(solution)/shard_map/ppermute | solution.py:12
  34.5 0.2 fusion.20
  34.7 0.4 fusion.25
  35.2 0.1 fusion.22
  35.3 0.0 copy-start
  35.4 0.7 copy-done
  36.4 85.5 %all-gather.2.cloned.1.call-done = bf16[6912,256]{0,1:T(8,128)(2,1)} async-done(((bf16[6912,16]{0,1:T(8,128)(2,1)}), bf16[6912,256]{0,1:T(8,128)(2,1)}) %all-gather.2.cloned.1.call-update) | async-done | bytes 3538960 | tf_op jit(solution)/shard_map/all_gather | solution.py:25
  122.0 1.8 %fusion = f32[256,256]{1,0:T(8,128)S(1)} fusion(bf16[256,2304]{1,0:T(8,128)(2,1)S(1)} %constant_dynamic-update-slice_fusion.21, bf16[6912,256]{0,1:T(8,128)(2,1)} %all-gather.2.cloned.1.call-done), kind=kOutput, calls=%fused_computation.2 | convolution fusion | flops 301989888 | bytes 2621440 | tf_op jit(solution)/shard_map/dot_general | solution.py:41
  123.7 1.8 %fusion.2 = f32[256,256]{1,0:T(8,128)S(1)} fusion(bf16[256,2304]{1,0:T(8,128)(2,1)S(1)} %constant_dynamic-update-slice_fusion.12, bf16[6912,256]{0,1:T(8,128)(2,1)} %all-gather.2.cloned.1.call-done), kind=kOutput, calls=%fused_computation.4 | convolution fusion | flops 301989888 | bytes 2621440 | tf_op jit(solution)/shard_map/dot_general | solution.py:41
  125.5 2.4 %fusion.13 = bf16[256,256]{1,0:T(8,128)(2,1)} fusion(f32[256,256]{1,0:T(8,128)S(1)} %fusion, f32[256,256]{1,0:T(8,128)S(1)} %fusion.2, bf16[256,2304]{1,0:T(8,128)(2,1)S(1)} %constant_dynamic-update-slice_fusion.3, bf16[6912,256]{0,1:T(8,128)(2,1)} %all-gather.2.cloned.1.call-done), kind=kOutput, calls=%fused_computation.11 | convolution fusion | flops 302186496 | bytes 3014656 | tf_op jit(solution)/shard_map/dot_general | solution.py:41
  (30 shorter events, 0.3 us)
Async XLA Ops:
  6.5 115.4 %all-gather.2.cloned.1.call-start = ((), (), s32[]{:S(2)}) async-start(), calls=%async_computation | async-start | bytes 3760128 | tf_op jit(solution)/shard_map/all_gather | solution.py:25
  8.1 6.8 %collective-permute-start = (bf16[1,2,64,256]{3,2,1,0:T(8,128)(2,1)S(1)}, bf16[1,2,64,256]{3,2,1,0:T(8,128)(2,1)S(1)}, u32[]{:S(2)}, u32[]{:S(2)}) collective-permute-start(bf16[1,2,64,256]{3,2,1,0:T(8,128)(2,1)S(1)} %get-tuple-element.38), channel_id=1, source_target_pairs={{0,48},{48,96},{96,144},{144,192},{192,240},{240,288},{288,336},{3... | collective-permute-start | bytes 196616 | tf_op jit(solution)/shard_map/ppermute | solution.py:12
  13.6 6.5 %collective-permute-start.1 = (bf16[1,2,64,256]{3,2,1,0:T(8,128)(2,1)S(1)}, bf16[1,2,64,256]{3,2,1,0:T(8,128)(2,1)S(1)}, u32[]{:S(2)}, u32[]{:S(2)}) collective-permute-start(bf16[1,2,64,256]{3,2,1,0:T(8,128)(2,1)S(1)} %get-tuple-element.37), channel_id=1, source_target_pairs={{48,0},{96,48},{144,96},{192,144},{240,192},{288,240},{336,288},{3... | collective-permute-start | bytes 196616 | tf_op jit(solution)/shard_map/ppermute | solution.py:15
  21.2 11.3 %collective-permute-start.3 = (bf16[4,1,64,256]{3,2,1,0:T(8,128)(2,1)S(1)}, bf16[4,1,64,256]{3,2,1,0:T(8,128)(2,1)S(1)}, u32[]{:S(2)}, u32[]{:S(2)}) collective-permute-start(bf16[4,1,64,256]{3,2,1,0:T(8,128)(2,1)S(1)} %get-tuple-element.33), channel_id=1, source_target_pairs={{1,0},{2,1},{3,2},{4,3},{5,4},{6,5},{7,6},{8,7},{9,8},{10,9},{11,1... | collective-permute-start | bytes 393224 | tf_op jit(solution)/shard_map/ppermute | solution.py:15
  30.6 3.9 %collective-permute-start.2 = (bf16[4,1,64,256]{3,2,1,0:T(8,128)(2,1)S(1)}, bf16[4,1,64,256]{3,2,1,0:T(8,128)(2,1)S(1)}, u32[]{:S(2)}, u32[]{:S(2)}) collective-permute-start(bf16[4,1,64,256]{3,2,1,0:T(8,128)(2,1)S(1)} %get-tuple-element.32), channel_id=1, source_target_pairs={{0,1},{1,2},{2,3},{3,4},{4,5},{5,6},{6,7},{7,8},{8,9},{9,10},{10,1... | collective-permute-start | bytes 393224 | tf_op jit(solution)/shard_map/ppermute | solution.py:12
  35.3 0.9 copy-start
Sparse Core Ops, SparseCore 0:
  11.1 110.8 all-gather.1
where the time goes:
time: 137 us; the launch traced here: 135 us
  waiting for transfers between devices  93.4 us (68%)
  starting transfers between devices  18.1 us (13%)
  between operations  13.7 us (10%)
  matrix products  5.98 us (4%)
  local copies, waits for them, and re-layouts  2.36 us (2%)
    all_gather x1, waiting for transfers between devices, local(): gathered = lax.all_gather(weights, 'slab', axis=1, tiled=True)  85.5 us
    ppermute x2, starting transfers between devices, extended_2(): lax.ppermute(lax.slice_in_dim(block, 0, width, axis=dim), axis, backward)  10.7 us
    ppermute x2, starting transfers between devices, extended_2(): lax.ppermute(lax.slice_in_dim(block, block.shape[dim] - width, None, axis...  7.4 us
    dot_general x3, matrix products, local(): jnp.dot(columns, kernel_rows, preferred_element_type=jnp.float32)  5.98 us
    ppermute x2, waiting for transfers between devices, extended_2(): lax.ppermute(lax.slice_in_dim(block, 0, width, axis=dim), axis, backward)  5.19 us
  transfers between devices with their start and end apart: 5, of which 3 were waited for; matrix products, arithmetic and copies ran while one was open for 2% of the time, Pallas kernels for 0%

commit v1 on v0

v1 whole, which is shorter than its diff:
```python
import functools

import jax
import jax.numpy as jnp
from jax import lax
from jax.experimental import pallas as pl
from jax.experimental.pallas import tpu as pltpu
from jax.sharding import PartitionSpec as P

MESH = pl.DeviceIdType.MESH
PIECES = (4, 4, 3, 3)
N = len(PIECES)
LAST = N - 1


def first_tap(i, half):
    low = sum(PIECES[:i])
    high = 13 if i == LAST else 13 + PIECES[LAST] + low
    return low + half * (high - low)


def other_taps(i):
    return PIECES[i] - 1 if i == LAST else PIECES[i]


def kernel(
    vol, w, out, *scratch
):
    a_bufs, b_bufs = scratch[:N], scratch[N : 2 * N]
    (halo, shifted, acc, own_a, own_b, swap_send, ring_send, ring_recv,
     z_send, z_recv, chip_send, chip_recv, halo_send, halo_recv, mid_sem) = scratch[2 * N :]
    s, ch = lax.axis_index("slab"), lax.axis_index("chan")
    y, xh = s // 2, s % 2
    core, xl, z = ch % 2, (ch // 2) % 2, ch // 4
    half = z % 2

    swap = (s + 1 - 2 * xh, ch + 2 - 4 * xl)
    ring = ((lax.rem(s + 2, 16), ch), (lax.rem(s + 14, 16), ch))
    zdev = ((s, lax.rem(ch + 4, 48)), (s, lax.rem(ch + 44, 48)))
    partner = (s, ch + 1 - 2 * core)
    s_up, s_dn = lax.rem(s + 1, 16), lax.rem(s + 15, 16)
    c_up, c_dn = lax.rem(ch + 1, 48), lax.rem(ch + 47, 48)
    halo_devs = (
        (s_up, ch), (s_dn, ch), (s, c_up), (s, c_dn),
        (s_up, c_up), (s_up, c_dn), (s_dn, c_up), (s_dn, c_dn),
    )

    barrier = pltpu.get_barrier_semaphore()
    greet = ring + zdev + (swap,) + halo_devs
    for dev in greet:
        pl.semaphore_signal(barrier, inc=1, device_id=dev, device_id_type=MESH)
    pl.semaphore_wait(barrier, len(greet))

    def rows(block, kind):
        return pl.ds(pl.multiple_of(block * 32 + kind * 16, 16), 16)

    def remote(src, dst, send, recv, dev):
        return pltpu.make_async_remote_copy(
            src_ref=src, dst_ref=dst, send_sem=send, recv_sem=recv,
            device_id=dev, device_id_type=MESH,
        )

    def lanes(start, taps):
        return pl.ds(pl.multiple_of(start * 256, 256), taps * 256)

    mine = rows(y, core)
    pltpu.make_async_copy(vol, halo.at[1:3, 1:3], mid_sem).start()

    def own_src(i, which):
        if which == 0:
            return w.at[:, lanes(first_tap(i, half), PIECES[i])]
        start = first_tap(i, 1 - half) + ((1 - half) if i == LAST else 0)
        return w.at[:, lanes(start, other_taps(i))]

    @pl.when(core == xh)
    def _():
        for which, bufs, sem in ((0, a_bufs, own_a), (1, b_bufs, own_b)):
            for i in range(N):
                src, dst = own_src(i, which), bufs[i].at[mine, :]
                remote(src, dst, swap_send.at[which, i], sem.at[i], swap).start()
                pltpu.make_async_copy(src, dst, sem.at[i]).start()

    sends = (
        (vol.at[1:2], halo.at[0:1, 1:3]),
        (vol.at[0:1], halo.at[3:4, 1:3]),
        (vol.at[:, 1:2], halo.at[1:3, 0:1]),
        (vol.at[:, 0:1], halo.at[1:3, 3:4]),
        (vol.at[1:2, 1:2], halo.at[0:1, 0:1]),
        (vol.at[1:2, 0:1], halo.at[0:1, 3:4]),
        (vol.at[0:1, 1:2], halo.at[3:4, 0:1]),
        (vol.at[0:1, 0:1], halo.at[3:4, 3:4]),
    )
    halo_copies = [
        remote(src, dst, halo_send, halo_recv.at[n], halo_devs[n])
        for n, (src, dst) in enumerate(sends)
    ]
    for copy in halo_copies:
        copy.start()

    def hops(d, k, i):
        return k < 3 or (k == 3 and (i % 2 == 0) == (d == 0))

    def block_of(d, k):
        return lax.rem(y + (7 - k if d == 0 else 1 + k), 8)

    def ring_copy(d, k, i):
        ref = a_bufs[i].at[rows(block_of(d, k - 1), core), :]
        return remote(ref, ref, ring_send.at[d, i], ring_recv.at[d, k, i], ring[d])

    def ring_wait(d, k, i):
        ref = a_bufs[i].at[rows(block_of(d, k), core), :]
        remote(ref, ref, ring_send.at[d, i], ring_recv.at[d, k, i], ring[d]).wait_recv()

    def z_copy(d, k, i):
        block = rows(block_of(d, k), core)
        if i == LAST:
            src = a_bufs[i].at[block, lanes(half, other_taps(i))]
        else:
            src = a_bufs[i].at[block, :]
        return remote(src, b_bufs[i].at[block, :], z_send.at[d, i], z_recv.at[d, k, i], zdev[d])

    def z_wait(d, k, i):
        ref = b_bufs[i].at[rows(block_of(d, k), core), :]
        remote(ref, ref, z_send.at[d, i], z_recv.at[d, k, i], zdev[d]).wait_recv()

    def chip_copy(which, block, i):
        ref = (a_bufs, b_bufs)[which][i].at[rows(block, core), :]
        return remote(ref, ref, chip_send.at[which, i], chip_recv.at[which, i], partner)

    def ring_events(k, i):
        for d in (0, 1):
            if hops(d, k, i):
                ring_wait(d, k, i)
                if hops(d, k + 1, i):
                    ring_copy(d, k + 1, i).start()
                z_copy(d, k, i).start()
                chip_copy(0, block_of(d, k), i).start()

    def z_events(k, i):
        for d in (0, 1):
            if hops(d, k, i):
                z_wait(d, k, i)
                chip_copy(1, block_of(d, k), i).start()

    def spread(d):
        for r in range(4):
            there = None
            if d == 0:
                there = s > 0
            if d == 3:
                there = s < 15
            if r == 0:
                there = (ch > 0) if there is None else there & (ch > 0)
            if r == 3:
                there = (ch < 47) if there is None else there & (ch < 47)
            plane = halo[d, r].astype(jnp.float32)
            if there is not None:
                plane = jnp.where(there, plane, 0.0)
            at = lax.broadcasted_iota(jnp.int32, plane.shape, 0)
            low = jnp.where(at == 0, 0.0, pltpu.roll(plane, 1, 0))
            high = jnp.where(at == 63, 0.0, pltpu.roll(plane, 63, 0))
            shifted[0, d, r] = low.astype(jnp.bfloat16)
            shifted[1, d, r] = plane.astype(jnp.bfloat16)
            shifted[2, d, r] = high.astype(jnp.bfloat16)

    def multiply(which, i):
        bufs = (a_bufs, b_bufs)[which]
        pltpu.make_async_copy(
            bufs[i].at[0:128, :], bufs[i].at[0:128, :], chip_recv.at[which, i]
        ).wait()
        if which == 0:
            start, count = first_tap(i, half), PIECES[i]
        else:
            count = other_taps(i)
            start = first_tap(i, 1 - half) + ((1 - half) if i == LAST else 0)
        taps = []
        for j in range(count):
            t = start + j
            a, b, e = t // 9, (t // 3) % 3, t % 3
            taps.append(
                jnp.concatenate(
                    [shifted[e, a + dd, b + rr] for dd in (0, 1) for rr in (0, 1)], axis=0
                )
            )
        left = jnp.concatenate(taps, axis=1)
        part = lax.dot_general(
            left, bufs[i][...], (((1,), (1,)), ((), ())), preferred_element_type=jnp.float32
        )
        if which == 0 and i == 0:
            acc[...] = part
        else:
            acc[...] += part

    for i in range(N):
        ref = a_bufs[i].at[mine, :]
        pltpu.make_async_copy(ref, ref, own_a.at[i]).wait()
        ring_copy(0, 0, i).start()
        ring_copy(1, 0, i).start()
        chip_copy(0, y, i).start()
    for k in range(4):
        if k == 2:
            for n, copy in enumerate(halo_copies):
                copy.wait_recv()
            pltpu.make_async_copy(vol, halo.at[1:3, 1:3], mid_sem).wait()
            for i in range(N):
                ref = b_bufs[i].at[mine, :]
                pltpu.make_async_copy(ref, ref, own_b.at[i]).wait()
                chip_copy(1, y, i).start()
        for i in range(N):
            ring_events(k, i)
            if k > 0:
                z_events(k - 1, i)
            if k == 2:
                for d in range(4 * i // N, 4 * (i + 1) // N):
                    spread(d)
    for i in range(N):
        multiply(0, i)
        z_events(3, i)
    for i in range(N):
        multiply(1, i)
    out[...] = acc[...].astype(jnp.bfloat16).reshape(out.shape)

    def drain(ref, sem):
        pltpu.make_async_copy(ref, ref, sem).wait()

    @pl.when(core == xh)
    def _():
        for which, bufs in ((0, a_bufs), (1, b_bufs)):
            for i in range(N):
                drain(bufs[i].at[0:16, :], swap_send.at[which, i])

    for i in range(N):
        for d in (0, 1):
            count = 3 + hops(d, 3, i)
            drain(a_bufs[i].at[0 : 16 * count, :], ring_send.at[d, i])
            drain(b_bufs[i].at[0 : 16 * count, :], z_send.at[d, i])
        drain(a_bufs[i].at[0:128, :], chip_send.at[0, i])
        drain(b_bufs[i].at[0:128, :], chip_send.at[1, i])
    drain(halo.at[0:3], halo_send)


def solution(mesh):
    def local(volume, weights):
        dma = pltpu.SemaphoreType.DMA
        return pl.pallas_call(
            kernel,
            out_shape=jax.ShapeDtypeStruct(volume.shape, jnp.bfloat16),
            in_specs=[pl.BlockSpec(memory_space=pl.ANY)] * 2,
            out_specs=pl.BlockSpec(memory_space=pltpu.VMEM),
            scratch_shapes=[pltpu.VMEM((256, 256 * n), jnp.bfloat16) for n in PIECES]
            + [pltpu.VMEM((256, 256 * other_taps(i)), jnp.bfloat16) for i in range(N)]
            + [
                pltpu.VMEM((4, 4, 64, 256), jnp.bfloat16),
                pltpu.VMEM((3, 4, 4, 64, 256), jnp.bfloat16),
                pltpu.VMEM((256, 256), jnp.float32),
                dma((N,)),
                dma((N,)),
                dma((2, N)),
                dma((2, N)),
                dma((2, 4, N)),
                dma((2, N)),
                dma((2, 4, N)),
                dma((2, N)),
                dma((2, N)),
                dma(()),
                dma((8,)),
                dma(()),
            ],
            compiler_params=pltpu.CompilerParams(collective_id=0, has_side_effects=True),
            name="conv_gather",
        )(volume, weights.T)

    return jax.shard_map(
        local,
        mesh=mesh,
        in_specs=(P("slab", "chan", None, None), P(None, "slab")),
        out_specs=P("slab", "chan", None, None),
        check_vma=False,
    )
```

time: 137 us -> 47.9 us (0.35)
  the two profiles are of different devices: /device:TPU:1 before, /device:TPU:7 now
where the time goes in v1:
time: 47.9 us; the launch traced here: 47.7 us
  Pallas kernels  46.2 us (96%)
  local copies, waits for them, and re-layouts  1.57 us (3%)
    pallas_call x1, Pallas kernels, local(): pl.pallas_call(kernel, out_shape=jax.ShapeDtypeStruct(volume.shape, jnp.b...  46.2 us
    unnamed x1, local copies, waits for them, and re-layouts  1.57 us

profile of v1, /device:TPU:7, one launch (start us, length us, event | category | flops | bytes accessed | tf_op | source)
XLA Modules:
  0.0 47.7 jit_solution(1636648049736324709)
XLA Ops:
  0.0 46.2 %conv_gather.1 = bf16[2,2,64,256]{3,2,1,0:T(8,128)(2,1)} custom-call(bf16[2,2,64,256]{3,2,1,0:T(8,128)(2,1)} %vol.1, bf16[16,6912]{1,0:T(8,128)(2,1)} %bitcast.1), custom_call_target="tpu_custom_call" | custom-call | tf_op jit(solution)/shard_map/conv_gather/pallas_call | solution.py:245
  46.2 1.6 %copy.4 = bf16[2,2,64,256]{3,2,1,0:T(8,128)(2,1)} copy(bf16[2,2,64,256]{3,2,1,0:T(8,128)(2,1)} %conv_gather.1) | data formatting | bytes 262144

commit v2 on v1

v2 whole, which is shorter than its diff:
```python
import jax
import jax.numpy as jnp
from jax import lax
from jax.experimental import pallas as pl
from jax.experimental.pallas import tpu as pltpu
from jax.sharding import PartitionSpec as P

MESH = pl.DeviceIdType.MESH
PIECES = (2, 2, 2, 2, 2, 2, 2)
N = len(PIECES)
LAST = N - 1
EDGE = (4, 5)
ZS = 12


def first_tap(i, half):
    low = sum(PIECES[:i])
    high = 13 if i == LAST else 13 + PIECES[LAST] + low
    return low + half * (high - low)


def other_taps(i):
    return PIECES[i] - 1 if i == LAST else PIECES[i]


def hops(d, k, i):
    return k < 3 or (k == 3 and (i % 2 == 0) == (d == 0))


def count(d, i):
    return 3 + hops(d, 3, i)


def kernel(vol, w, out, *scratch):
    a_bufs, b_bufs = scratch[:N], scratch[N : 2 * N]
    (halo, shifted, acc, own, swap_send, ring_send, ring_recv, z_send, z_recv, edge_send,
     chip_send, chip_recv, halo_send, halo_recv, mid_sem, near_sem, far_sem) = scratch[2 * N :]
    bufs = (a_bufs, b_bufs)
    s, ch = lax.axis_index("slab"), lax.axis_index("chan")
    y, xh = s // 2, s % 2
    core, xl, z = ch % 2, (ch // 2) % 2, ch // 4
    half = z % 2
    at_edge = (z == 0) | (z == ZS - 1)

    swap = (s + 1 - 2 * xh, ch + 2 - 4 * xl)
    across = (s, ch + 2 - 4 * xl)
    ring = ((lax.rem(s + 2, 16), ch), (lax.rem(s + 14, 16), ch))
    zdev = ((s, jnp.minimum(ch + 4, 47)), (s, jnp.maximum(ch - 4, 0)))
    has_z = (z < ZS - 1, z > 0)
    partner = (s, ch + 1 - 2 * core)
    depth_dev = ((lax.rem(s + 1, 16), ch), (lax.rem(s + 15, 16), ch))
    row_dev = ((s, jnp.minimum(ch + 1, 47)), (s, jnp.maximum(ch - 1, 0)))
    has_row = (ch < 47, ch > 0)
    n_near = 5 + jnp.where(z < ZS - 1, 1, 0) + jnp.where(z > 0, 1, 0)

    def greet(sem):
        for dev in ring + (swap, across, partner):
            pl.semaphore_signal(sem, inc=1, device_id=dev, device_id_type=MESH)
        for d in (0, 1):

            @pl.when(has_z[d])
            def _():
                pl.semaphore_signal(sem, inc=1, device_id=zdev[d], device_id_type=MESH)

    barrier = pltpu.get_barrier_semaphore()
    greet(barrier)
    pl.semaphore_wait(barrier, n_near)

    def rows(block, kind):
        return pl.ds(pl.multiple_of(block * 32 + kind * 16, 16), 16)

    def remote(src, dst, send, recv, dev):
        return pltpu.make_async_remote_copy(
            src_ref=src, dst_ref=dst, send_sem=send, recv_sem=recv,
            device_id=dev, device_id_type=MESH,
        )

    def lanes(start, taps):
        return pl.ds(pl.multiple_of(start * 256, 256), taps * 256)

    def taps_of(which, i):
        if which == 0:
            return first_tap(i, half), PIECES[i]
        return first_tap(i, 1 - half) + ((1 - half) if i == LAST else 0), other_taps(i)

    def land(sem, ref):
        pltpu.make_async_copy(ref, ref, sem).wait()

    def block_of(d, k):
        return lax.rem(y + (7 - k if d == 0 else 1 + k), 8)

    def ring_copy(d, k, i, src=None):
        ref = a_bufs[i].at[rows(block_of(d, k - 1), core), :]
        return remote(ref if src is None else src, ref, ring_send.at[d, i], ring_recv.at[d, k, i], ring[d])

    def edge_copy(d, k, i, src=None):
        ref = b_bufs[i].at[rows(block_of(d, k - 1), core), :]
        return remote(ref if src is None else src, ref, edge_send.at[d, i], z_recv.at[d, k, i], ring[d])

    def z_copy(d, k, i, to):
        block = rows(block_of(d, k), core)
        if i == LAST:
            src = a_bufs[i].at[block, lanes(half, other_taps(i))]
        else:
            src = a_bufs[i].at[block, :]
        return remote(src, b_bufs[i].at[block, :], z_send.at[to, i], z_recv.at[d, k, i], zdev[to])

    def chip_copy(which, block, i, src=None):
        ref = bufs[which][i].at[rows(block, core), :]
        return remote(
            ref if src is None else src, ref, chip_send.at[which, i], chip_recv.at[which, i], partner
        )

    mine = rows(y, core)

    def own_src(which, i):
        start, taps = taps_of(which, i)
        return w.at[:, lanes(start, taps)]

    greet(near_sem)

    @pl.when(core == xh)
    def _():
        for i in range(N):
            src = own_src(0, i)
            remote(src, a_bufs[i].at[mine, :], swap_send.at[0, i], own.at[0, i], swap).start()
            for d in (0, 1):
                ring_copy(d, 0, i, src).start()
        for i in range(N):
            src = own_src(1, i)
            remote(src, b_bufs[i].at[mine, :], swap_send.at[1, i], own.at[1, i], swap).start()
            if i in EDGE:

                @pl.when(at_edge)
                def _():
                    for d in (0, 1):
                        edge_copy(d, 0, i, src).start()

        for which in (0, 1):
            for i in range(N):
                src = own_src(which, i)
                chip_copy(which, y, i, src).start()
                pltpu.make_async_copy(src, bufs[which][i].at[mine, :], own.at[which, i]).start()

    pltpu.make_async_copy(vol, halo.at[1:3, 1:3], mid_sem).start()
    pl.semaphore_wait(near_sem, n_near)
    greet(far_sem)
    pl.semaphore_wait(far_sem, n_near)

    depth_copies = [
        remote(vol.at[1:2], halo.at[0:1, 1:3], halo_send.at[0], halo_recv.at[0], depth_dev[0]),
        remote(vol.at[0:1], halo.at[3:4, 1:3], halo_send.at[1], halo_recv.at[1], depth_dev[1]),
    ]
    row_copies = [
        remote(halo.at[:, 2:3], halo.at[:, 0:1], halo_send.at[2], halo_recv.at[2], row_dev[0]),
        remote(halo.at[:, 1:2], halo.at[:, 3:4], halo_send.at[3], halo_recv.at[3], row_dev[1]),
    ]
    for copy in depth_copies:
        copy.start()

    @pl.when(core != xh)
    def _():
        for i in range(N):
            land(own.at[0, i], a_bufs[i].at[mine, :])
            for d in (0, 1):
                ring_copy(d, 0, i, a_bufs[i].at[mine, :]).start()
            chip_copy(0, y, i).start()

    def ring_events(k, i):
        for d in (0, 1):
            if not hops(d, k, i):
                continue
            ref = a_bufs[i].at[rows(block_of(d, k), core), :]
            remote(ref, ref, ring_send.at[d, i], ring_recv.at[d, k, i], ring[d]).wait_recv()
            if hops(d, k + 1, i):
                ring_copy(d, k + 1, i).start()
            toward = (z == ZS - 2) if d == 0 else (z == 1)
            away = (z == 1) if d == 0 else (z == ZS - 2)
            plain = has_z[d] & jnp.logical_not(toward) if i in EDGE else has_z[d]

            @pl.when(plain)
            def _():
                z_copy(d, k, i, d).start()

            if i not in EDGE:

                @pl.when(away)
                def _():
                    z_copy(d, k, i, 1 - d).start()

            chip_copy(0, block_of(d, k), i).start()

    def z_events(k, i):
        for d in (0, 1):
            if not hops(d, k, i):
                continue
            ref = b_bufs[i].at[rows(block_of(d, k), core), :]
            remote(ref, ref, z_send.at[d, i], z_recv.at[d, k, i], zdev[d]).wait_recv()
            if i in EDGE and hops(d, k + 1, i):

                @pl.when(at_edge)
                def _():
                    edge_copy(d, k + 1, i).start()

            chip_copy(1, block_of(d, k), i).start()

    def spread(d):
        for r in range(4):
            there = []
            if d == 0:
                there.append(s > 0)
            if d == 3:
                there.append(s < 15)
            if r == 0:
                there.append(ch > 0)
            if r == 3:
                there.append(ch < 47)
            plane = halo[d, r].astype(jnp.float32)
            for cond in there:
                plane = jnp.where(cond, plane, 0.0)
            at = lax.broadcasted_iota(jnp.int32, plane.shape, 0)
            low = jnp.where(at == 0, 0.0, pltpu.roll(plane, 1, 0))
            high = jnp.where(at == 63, 0.0, pltpu.roll(plane, 63, 0))
            shifted[0, d, r] = low.astype(jnp.bfloat16)
            shifted[1, d, r] = plane.astype(jnp.bfloat16)
            shifted[2, d, r] = high.astype(jnp.bfloat16)

    def multiply(which, i):
        buf = bufs[which][i]
        land(chip_recv.at[which, i], buf.at[0:128, :])
        start, number = taps_of(which, i)
        taps = []
        for j in range(number):
            t = start + j
            a, b, e = t // 9, (t // 3) % 3, t % 3
            taps.append(
                jnp.concatenate(
                    [shifted[e, a + dd, b + rr] for dd in (0, 1) for rr in (0, 1)], axis=0
                )
            )
        left = jnp.concatenate(taps, axis=1)
        part = lax.dot_general(
            left, buf[...], (((1,), (1,)), ((), ())), preferred_element_type=jnp.float32
        )
        if which == 0 and i == 0:
            acc[...] = part
        else:
            acc[...] += part

    for k in range(4):
        for i in range(N):
            ring_events(k, i)
            if k > 0:
                z_events(k - 1, i)
            if k == 3 and i < 4:
                spread(i)
        if k == 0:

            @pl.when(core != xh)
            def _():
                for i in range(N):
                    land(own.at[1, i], b_bufs[i].at[mine, :])
                    chip_copy(1, y, i).start()
                    if i in EDGE:

                        @pl.when(at_edge)
                        def _():
                            for d in (0, 1):
                                edge_copy(d, 0, i, b_bufs[i].at[mine, :]).start()

        if k == 1:
            for copy in depth_copies:
                copy.wait_recv()
            land(mid_sem, halo.at[1:3, 1:3])
            for d in (0, 1):

                @pl.when(has_row[d])
                def _():
                    row_copies[d].start()

        if k == 2:
            for d in (0, 1):

                @pl.when(has_row[1 - d])
                def _():
                    row_copies[d].wait_recv()

            @pl.when(core == xh)
            def _():
                for which in (0, 1):
                    for i in range(N):
                        land(own.at[which, i], bufs[which][i].at[mine, :])

    for i in range(N):
        multiply(0, i)
        z_events(3, i)
    for i in range(N):
        multiply(1, i)
    out[...] = acc[...].astype(jnp.bfloat16).reshape(out.shape)

    def left(buf, blocks, sem):
        land(sem, buf.at[0 : 16 * blocks, :])

    @pl.when(core == xh)
    def _():
        for which in (0, 1):
            for i in range(N):
                left(bufs[which][i], 1, swap_send.at[which, i])

    for i in range(N):
        both = count(0, i) + count(1, i)
        for d in (0, 1):
            left(a_bufs[i], count(d, i), ring_send.at[d, i])
            toward = (z == ZS - 2) if d == 0 else (z == 1)

            @pl.when(has_z[d] & jnp.logical_not(toward))
            def _():
                left(b_bufs[i], count(d, i), z_send.at[d, i])

            if i not in EDGE:

                @pl.when(toward)
                def _():
                    left(b_bufs[i], both, z_send.at[d, i])

            else:

                @pl.when(at_edge)
                def _():
                    left(b_bufs[i], count(d, i), edge_send.at[d, i])

        for which in (0, 1):
            left(bufs[which][i], 8, chip_send.at[which, i])
    for copy in depth_copies:
        copy.wait_send()
    for d in (0, 1):

        @pl.when(has_row[d])
        def _():
            row_copies[d].wait_send()


def solution(mesh):
    def local(volume, weights):
        dma, regular = pltpu.SemaphoreType.DMA, pltpu.SemaphoreType.REGULAR
        return pl.pallas_call(
            kernel,
            out_shape=jax.ShapeDtypeStruct(volume.shape, jnp.bfloat16),
            in_specs=[pl.BlockSpec(memory_space=pl.ANY)] * 2,
            out_specs=pl.BlockSpec(memory_space=pltpu.VMEM),
            scratch_shapes=[pltpu.VMEM((256, 256 * n), jnp.bfloat16) for n in PIECES]
            + [pltpu.VMEM((256, 256 * other_taps(i)), jnp.bfloat16) for i in range(N)]
            + [
                pltpu.VMEM((4, 4, 64, 256), jnp.bfloat16),
                pltpu.VMEM((3, 4, 4, 64, 256), jnp.bfloat16),
                pltpu.VMEM((256, 256), jnp.float32),
                dma((2, N)),
                dma((2, N)),
                dma((2, N)),
                dma((2, 4, N)),
                dma((2, N)),
                dma((2, 4, N)),
                dma((2, N)),
                dma((2, N)),
                dma((2, N)),
                dma((4,)),
                dma((4,)),
                dma(()),
                regular,
                regular,
            ],
            compiler_params=pltpu.CompilerParams(collective_id=0, has_side_effects=True),
            name="conv_gather",
        )(volume, weights.T)

    return jax.shard_map(
        local,
        mesh=mesh,
        in_specs=(P("slab", "chan", None, None), P(None, "slab")),
        out_specs=P("slab", "chan", None, None),
        check_vma=False,
    )
```

time: 47.9 us -> 39.3 us (0.82)
  the two profiles are of different devices: /device:TPU:7 before, /device:TPU:1 now
where the time goes in v2:
time: 39.3 us; the launch traced here: 39.2 us
  Pallas kernels  37.6 us (96%)
  local copies, waits for them, and re-layouts  1.57 us (4%)
    pallas_call x1, Pallas kernels, local(): pl.pallas_call(kernel, out_shape=jax.ShapeDtypeStruct(volume.shape, jnp.b...  37.6 us
    unnamed x1, local copies, waits for them, and re-layouts  1.57 us

profile of v2, /device:TPU:1, one launch (start us, length us, event | category | flops | bytes accessed | tf_op | source)
XLA Modules:
  0.0 39.2 jit_solution(678081245870252790)
XLA Ops:
  0.0 37.6 %conv_gather.1 = bf16[2,2,64,256]{3,2,1,0:T(8,128)(2,1)} custom-call(bf16[2,2,64,256]{3,2,1,0:T(8,128)(2,1)} %vol.1, bf16[16,6912]{1,0:T(8,128)(2,1)} %bitcast.1), custom_call_target="tpu_custom_call" | custom-call | tf_op jit(solution)/shard_map/conv_gather/pallas_call | solution.py:346
  37.6 1.6 %copy.4 = bf16[2,2,64,256]{3,2,1,0:T(8,128)(2,1)} copy(bf16[2,2,64,256]{3,2,1,0:T(8,128)(2,1)} %conv_gather.1) | data formatting | bytes 262144

commit v3 on v0

v3 whole, which is shorter than its diff:
```python
import jax
import jax.numpy as jnp
from jax import lax
from jax.experimental import pallas as pl
from jax.experimental.pallas import tpu as pltpu
from jax.sharding import PartitionSpec as P

MESH = pl.DeviceIdType.MESH
PIECES = (7, 7)
N = len(PIECES)
LAST = N - 1
ZS = 12
LAG = 2


def first_tap(i, half):
    low = sum(PIECES[:i])
    high = 13 if i == LAST else 13 + PIECES[LAST] + low
    return low + half * (high - low)


def other_taps(i):
    return PIECES[i] - 1 if i == LAST else PIECES[i]


def hops(d, k, i):
    return k < 3 or (k == 3 and (i % 2 == 0) == (d == 0))


def count(d, i):
    return 3 + hops(d, 3, i)


def kernel(vol, w, out, *scratch):
    a_bufs, b_bufs = scratch[:N], scratch[N : 2 * N]
    (halo, shifted, acc, own, swap_send, ring_send, ring_recv, z_send, z_recv,
     chip_send, chip_recv, halo_send, halo_recv, mid_sem, near_sem, far_sem, late_sem) = scratch[2 * N :]
    bufs = (a_bufs, b_bufs)
    s, ch = lax.axis_index("slab"), lax.axis_index("chan")
    y, xh = s // 2, s % 2
    core, xl, z = ch % 2, (ch // 2) % 2, ch // 4
    half = z % 2
    is_late = (s == 0) & (ch == 0)
    is_host = (s == 0) & (ch == 1)
    meets_late = (s == 1) & (ch == 0)
    active = jnp.logical_not(is_late)
    plain = jnp.logical_not((s == 0) & (ch < 2))
    here = core == xh

    def host(dev):
        return dev[0], jnp.where((dev[0] == 0) & (dev[1] == 0), 1, dev[1])

    def seat(kind):
        return ch - core + kind

    def ring_dev(d, kind):
        return host((lax.rem(s + (2 if d == 0 else 14), 16), seat(kind)))

    def swap_dev(kind):
        return host((s + 1 - 2 * xh, seat(kind) + 2 - 4 * xl))

    def z_dev(d, kind):
        c = seat(kind)
        return host((s, jnp.minimum(c + 4, 47) if d == 0 else jnp.maximum(c - 4, 0)))

    def devices(kind):
        return (
            (ring_dev(0, kind), ring_dev(1, kind)), swap_dev(kind),
            (z_dev(0, kind), z_dev(1, kind)), host((s, seat(kind) + 2 - 4 * xl)),
        )

    own_devices, zero_devices = devices(core), devices(0)

    def ring_of(kind):
        return (own_devices if kind is core else zero_devices)[0]

    def swap_of(kind):
        return (own_devices if kind is core else zero_devices)[1]

    def z_of(kind):
        return (own_devices if kind is core else zero_devices)[2]

    def across_of(kind):
        return (own_devices if kind is core else zero_devices)[3]

    partner = (s, ch + 1 - 2 * core)
    has_z = (z < ZS - 1, z > 0)
    depth_dev = ((jnp.minimum(s + 1, 15), ch), (jnp.maximum(s - 1, 0), ch))
    has_depth = (s < 15, s > 0)
    row_dev = ((s, jnp.minimum(ch + 1, 47)), (s, jnp.maximum(ch - 1, 0)))
    has_row = (ch < 47, ch > 0)

    def signal(sem, dev):
        pl.semaphore_signal(sem, inc=1, device_id=dev, device_id_type=MESH)

    def greet_as(sem, kind):
        for d in (0, 1):
            signal(sem, ring_of(kind)[d])
        signal(sem, swap_of(kind))
        signal(sem, across_of(kind))

    def greet(sem):
        greet_as(sem, core)

        @pl.when(plain)
        def _():
            signal(sem, partner)

        @pl.when(is_host)
        def _():
            greet_as(sem, 0)

    n_plane = jnp.where(is_host, 8, 5)
    n_z = has_z[0].astype(jnp.int32) + has_z[1].astype(jnp.int32)

    barrier = pltpu.get_barrier_semaphore()

    @pl.when(active)
    def _():
        greet(barrier)

    def greet_z(kind):
        for d in (0, 1):

            @pl.when(has_z[d])
            def _():
                signal(barrier, z_of(kind)[d])

    @pl.when(active)
    def _():
        greet_z(core)

    @pl.when(is_host)
    def _():
        greet_z(0)

    @pl.when(is_host | meets_late)
    def _():
        signal(barrier, (0, 0))

    pl.semaphore_wait(barrier, jnp.where(is_late, 2, n_plane + n_z * jnp.where(is_host, 2, 1)))

    @pl.when(is_late)
    def _():
        signal(late_sem, (0, 1))
        signal(late_sem, (1, 0))

    def remote(src, dst, send, recv, dev):
        return pltpu.make_async_remote_copy(
            src_ref=src, dst_ref=dst, send_sem=send, recv_sem=recv,
            device_id=dev, device_id_type=MESH,
        )

    def lanes(start, taps):
        return pl.ds(pl.multiple_of(start * 256, 256), taps * 256)

    def taps_of(which, i):
        if which == 0:
            return first_tap(i, half), PIECES[i]
        return first_tap(i, 1 - half) + ((1 - half) if i == LAST else 0), other_taps(i)

    def land(sem, ref):
        pltpu.make_async_copy(ref, ref, sem).wait()

    blocks = [[lax.rem(y + (7 - k if d == 0 else 1 + k), 8) for k in range(4)] for d in (0, 1)]

    def block_of(d, k):
        return y if k < 0 else blocks[d][k]

    def ring_copy(d, k, i, kind, src=None):
        ref = a_bufs[i].at[block_of(d, k - 1), kind]
        return remote(
            ref if src is None else src, ref,
            ring_send.at[kind, d, i], ring_recv.at[kind, d, k, i], ring_of(kind)[d],
        )

    def z_copy(d, k, i, to, kind):
        block = block_of(d, k)
        if i == LAST:
            src = a_bufs[i].at[block, kind, :, lanes(half, other_taps(i))]
        else:
            src = a_bufs[i].at[block, kind]
        return remote(
            src, b_bufs[i].at[block, kind],
            z_send.at[kind, to, i], z_recv.at[kind, d, k, i], z_of(kind)[to],
        )

    def chip_give(which, i):
        @pl.when(plain)
        def _():
            ref = bufs[which][i].at[:, core]
            remote(ref, ref, chip_send.at[which, i], chip_recv.at[which, i], partner).start()

    def host_give(which, i, early):
        for part in ((slice(0, 4), slice(5, 8)) if early else (slice(4, 5),)):
            ref = bufs[which][i].at[part]
            remote(ref, ref, chip_send.at[which, i], chip_recv.at[which, i], partner).start()

    def own_src(which, i):
        start, taps = taps_of(which, i)
        return w.at[:, lanes(start, taps)]

    def give_a(kind):
        for i in range(N):
            src, mine = own_src(0, i), a_bufs[i].at[y, kind]
            remote(src, mine, swap_send.at[kind, 0, i], own.at[kind, 0, i], swap_of(kind)).start()
            for d in (0, 1):
                ring_copy(d, 0, i, kind, src).start()

    def give_b(kind):
        for i in range(N):
            src, mine = own_src(1, i), b_bufs[i].at[y, kind]
            remote(src, mine, swap_send.at[kind, 1, i], own.at[kind, 1, i], swap_of(kind)).start()

    def keep(kind):
        for which in (0, 1):
            for i in range(N):
                src, mine = own_src(which, i), bufs[which][i].at[y, kind]
                pltpu.make_async_copy(src, mine, own.at[kind, which, i]).start()

    def ring_events(k, i, kind):
        for d in (0, 1):
            if not hops(d, k, i):
                continue
            land(ring_recv.at[kind, d, k, i], a_bufs[i].at[block_of(d, k), kind])
            if hops(d, k + 1, i):
                ring_copy(d, k + 1, i, kind).start()
            away = (z == 1) if d == 0 else (z == ZS - 2)

            @pl.when(has_z[d])
            def _():
                z_copy(d, k, i, d, kind).start()

            @pl.when(away)
            def _():
                z_copy(d, k, i, 1 - d, kind).start()

    def z_events(k, i, kind):
        for d in (0, 1):
            if not hops(d, k, i):
                continue
            land(z_recv.at[kind, d, k, i], b_bufs[i].at[block_of(d, k), kind])

    depth_copies = [
        remote(vol.at[1:2], halo.at[0:1, 1:3], halo_send.at[0], halo_recv.at[0], depth_dev[0]),
        remote(vol.at[0:1], halo.at[3:4, 1:3], halo_send.at[1], halo_recv.at[1], depth_dev[1]),
    ]
    row_copies = [
        remote(halo.at[:, 2:3], halo.at[:, 0:1], halo_send.at[2], halo_recv.at[2], row_dev[0]),
        remote(halo.at[:, 1:2], halo.at[:, 3:4], halo_send.at[3], halo_recv.at[3], row_dev[1]),
    ]

    def halo_rows():
        for d in (0, 1):

            @pl.when(has_depth[1 - d])
            def _():
                depth_copies[d].wait_recv()

        land(mid_sem, halo.at[1:3, 1:3])
        for d in (0, 1):
            wanted = has_row[d] if d == 0 else has_row[d] & jnp.logical_not(is_host)

            @pl.when(wanted)
            def _():
                row_copies[d].start()

    def spread(d):
        for r in range(4):
            there = []
            if d == 0:
                there.append(s > 0)
            if d == 3:
                there.append(s < 15)
            if r == 0:
                there.append(ch > 0)
            if r == 3:
                there.append(ch < 47)
            x = halo[d, r].astype(jnp.float32)
            for cond in there:
                x = jnp.where(cond, x, 0.0)
            at = lax.broadcasted_iota(jnp.int32, x.shape, 0)
            low = jnp.where(at == 0, 0.0, pltpu.roll(x, 1, 0))
            high = jnp.where(at == 63, 0.0, pltpu.roll(x, 63, 0))
            shifted[0, d, r] = low.astype(jnp.bfloat16)
            shifted[1, d, r] = x.astype(jnp.bfloat16)
            shifted[2, d, r] = high.astype(jnp.bfloat16)

    def multiply(which, i):
        buf = bufs[which][i]

        @pl.when(plain)
        def _():
            land(chip_recv.at[which, i], buf.at[:, core])

        @pl.when(is_late)
        def _():
            land(chip_recv.at[which, i], buf)

        start, number = taps_of(which, i)
        taps = []
        for j in range(number):
            t = start + j
            a, b, e = t // 9, (t // 3) % 3, t % 3
            taps.append(
                jnp.concatenate(
                    [shifted[e, a + dd, b + rr] for dd in (0, 1) for rr in (0, 1)], axis=0
                )
            )
        left = jnp.concatenate(taps, axis=1)
        part = lax.dot_general(
            left, buf[...].reshape(256, 256 * number), (((1,), (1,)), ((), ())), preferred_element_type=jnp.float32
        )
        if which == 0 and i == 0:
            acc[...] = part
        else:
            acc[...] += part

    pltpu.make_async_copy(vol, halo.at[1:3, 1:3], mid_sem).start()

    @pl.when(is_late)
    def _():
        depth_copies[0].start()
        halo_rows()

    @pl.when(active)
    def _():
        greet(near_sem)

        @pl.when(is_host)
        def _():
            give_a(0)

        @pl.when(here)
        def _():
            give_a(core)
            give_b(core)
            keep(core)

        @pl.when(is_host)
        def _():
            give_b(0)
            keep(0)

        @pl.when(jnp.logical_not(here))
        def _():
            for i in range(N):
                land(own.at[core, 0, i], a_bufs[i].at[y, core])
                for d in (0, 1):
                    ring_copy(d, 0, i, core, a_bufs[i].at[y, core]).start()

        pl.semaphore_wait(near_sem, n_plane)
        greet(far_sem)
        for k in range(4):
            for i in range(N):
                ring_events(k, i, core)

                @pl.when(is_host)
                def _():
                    ring_events(k, i, 0)

                if k == 3:

                    @pl.when(plain)
                    def _():
                        chip_give(0, i)

                if k >= LAG:
                    z_events(k - LAG, i, core)
            if k == 0:
                pl.semaphore_wait(far_sem, n_plane)
                for d in (0, 1):
                    wanted = has_depth[d] if d == 0 else has_depth[d] & jnp.logical_not(meets_late)

                    @pl.when(wanted)
                    def _():
                        depth_copies[d].start()

                @pl.when(here)
                def _():
                    for which in (0, 1):
                        for i in range(N):
                            land(own.at[core, which, i], bufs[which][i].at[y, core])

                @pl.when(jnp.logical_not(here))
                def _():
                    for i in range(N):
                        land(own.at[core, 1, i], b_bufs[i].at[y, core])

            if k == 2:

                @pl.when(meets_late)
                def _():
                    pl.semaphore_wait(late_sem, 1)
                    depth_copies[1].start()

                @pl.when(jnp.logical_not(meets_late))
                def _():
                    halo_rows()

                @pl.when(is_host)
                def _():
                    pl.semaphore_wait(late_sem, 1)
                    row_copies[1].start()
                    for which in (0, 1):
                        for i in range(N):
                            land(own.at[0, which, i], bufs[which][i].at[y, 0])
                    for i in range(N):
                        host_give(0, i, True)

        @pl.when(meets_late)
        def _():
            halo_rows()

        @pl.when(is_host)
        def _():
            for i in range(N):
                host_give(0, i, False)

        for k in range(4 - LAG, 3):
            for i in range(N):
                z_events(k, i, core)

        @pl.when(is_host)
        def _():
            for i in range(N):
                for k in range(3):
                    z_events(k, i, 0)
                host_give(1, i, True)

    for d in (0, 1):

        @pl.when(has_row[1 - d])
        def _():
            row_copies[d].wait_recv()

    for d in range(4):
        spread(d)
    for i in range(N):
        multiply(0, i)

        @pl.when(active)
        def _():
            z_events(3, i, core)

        @pl.when(is_host)
        def _():
            z_events(3, i, 0)
            host_give(1, i, False)

        chip_give(1, i)

    for i in range(N):
        multiply(1, i)
    out[...] = acc[...].astype(jnp.bfloat16).reshape(out.shape)

    def left(buf, blocks, sem):
        land(sem, buf if blocks == 16 else buf.at[0:blocks, 0])

    def gone(kind):
        for i in range(N):
            both = count(0, i) + count(1, i)
            for d in (0, 1):
                left(a_bufs[i], count(d, i), ring_send.at[kind, d, i])
                toward = (z == ZS - 2) if d == 0 else (z == 1)

                @pl.when(has_z[d] & jnp.logical_not(toward))
                def _():
                    left(b_bufs[i], count(d, i), z_send.at[kind, d, i])

                @pl.when(toward)
                def _():
                    left(b_bufs[i], both, z_send.at[kind, d, i])

    def gone_own(kind):
        for which in (0, 1):
            for i in range(N):
                left(bufs[which][i], 1, swap_send.at[kind, which, i])

    @pl.when(active)
    def _():
        gone(core)

        @pl.when(here)
        def _():
            gone_own(core)

    @pl.when(is_host)
    def _():
        gone(0)
        gone_own(0)
        for which in (0, 1):
            for i in range(N):
                left(bufs[which][i], 16, chip_send.at[which, i])

    @pl.when(plain)
    def _():
        for which in (0, 1):
            for i in range(N):
                left(bufs[which][i], 8, chip_send.at[which, i])

    for d in (0, 1):

        @pl.when(has_depth[d])
        def _():
            depth_copies[d].wait_send()

        @pl.when(has_row[d])
        def _():
            row_copies[d].wait_send()


def solution(mesh):
    def local(volume, weights):
        dma, regular = pltpu.SemaphoreType.DMA, pltpu.SemaphoreType.REGULAR
        return pl.pallas_call(
            kernel,
            out_shape=pltpu.VMEM(volume.shape, jnp.bfloat16),
            in_specs=[pl.BlockSpec(memory_space=pl.ANY)] * 2,
            out_specs=pl.BlockSpec(memory_space=pltpu.VMEM),
            scratch_shapes=[pltpu.VMEM((8, 2, 16, 256 * n), jnp.bfloat16) for n in PIECES]
            + [pltpu.VMEM((8, 2, 16, 256 * other_taps(i)), jnp.bfloat16) for i in range(N)]
            + [
                pltpu.VMEM((4, 4, 64, 256), jnp.bfloat16),
                pltpu.VMEM((3, 4, 4, 64, 256), jnp.bfloat16),
                pltpu.VMEM((256, 256), jnp.float32),
                dma((2, 2, N)),
                dma((2, 2, N)),
                dma((2, 2, N)),
                dma((2, 2, 4, N)),
                dma((2, 2, N)),
                dma((2, 2, 4, N)),
                dma((2, N)),
                dma((2, N)),
                dma((4,)),
                dma((4,)),
                dma(()),
                regular,
                regular,
                regular,
            ],
            compiler_params=pltpu.CompilerParams(collective_id=0, has_side_effects=True),
            name="conv_gather",
        )(volume, weights.T)

    return jax.shard_map(
        local,
        mesh=mesh,
        in_specs=(P("slab", "chan", None, None), P(None, "slab")),
        out_specs=P("slab", "chan", None, None),
        check_vma=False,
    )
```

time: 137 us -> 34.6 us (0.25); the launches traced: 135 us -> 34.5 us
  waiting for transfers between devices: 93.4 us -> 0 us
  Pallas kernels: 0 us -> 33.8 us
  starting transfers between devices: 18.1 us -> 0 us
  between operations: 13.7 us -> 0.01 us
  matrix products: 5.98 us -> 0 us
  local copies, waits for them, and re-layouts: 2.36 us -> 0.66 us
    all_gather x1 -> x0, waiting for transfers between devices: 85.5 us -> none  [local(): gathered = lax.all_gather(weights, 'slab', axis=1, tiled=True)]
    pallas_call x0 -> x1, Pallas kernels: none -> 33.8 us  [local(): pl.pallas_call(kernel, out_shape=pltpu.VMEM(volume.shape, jnp.bfloat16),...]
    ppermute x4 -> x0, starting transfers between devices: 18.1 us -> none  [the longest x2 10.7 us: extended_2(): lax.ppermute(lax.slice_in_dim(block, 0, width, axis=dim), axis, backward)]
    ppermute x4 -> x0, waiting for transfers between devices: 7.12 us -> none  [the longest x2 5.19 us: extended_2(): lax.ppermute(lax.slice_in_dim(block, 0, width, axis=dim), axis, backward)]
    dot_general x3 -> x0, matrix products: 5.98 us -> none  [local(): jnp.dot(columns, kernel_rows, preferred_element_type=jnp.float32)]
  transfers between devices with their start and end apart: 5 -> 0, of which waited for: 3 -> 0; matrix products, arithmetic and copies ran while one was open for 2% -> 0% of each run, Pallas kernels for 0% -> 0%
where the time goes in v3:
time: 34.6 us; the launch traced here: 34.5 us
  Pallas kernels  33.8 us (98%)
  local copies, waits for them, and re-layouts  0.66 us (2%)
    pallas_call x1, Pallas kernels, local(): pl.pallas_call(kernel, out_shape=pltpu.VMEM(volume.shape, jnp.bfloat16),...  33.8 us

profile of v3, /device:TPU:1, one launch (start us, length us, event | category | flops | bytes accessed | tf_op | source)
XLA Modules:
  0.0 34.5 jit_solution(16734648011568850811)
XLA Ops:
  0.0 33.8 %conv_gather.1 = bf16[2,2,64,256]{3,2,1,0:T(8,128)(2,1)S(1)} custom-call(bf16[2,2,64,256]{3,2,1,0:T(8,128)(2,1)} %vol.1, bf16[16,6912]{1,0:T(8,128)(2,1)} %bitcast.1), custom_call_target="tpu_custom_call" | custom-call | tf_op jit(solution)/shard_map/conv_gather/pallas_call | solution.py:516
  33.8 0.7 %copy.4 = bf16[2,2,64,256]{3,2,1,0:T(8,128)(2,1)} copy(bf16[2,2,64,256]{3,2,1,0:T(8,128)(2,1)S(1)} %conv_gather.1) | data formatting | bytes 262144

commit v4 on v3

--- a/solution.py
+++ b/solution.py
@@ -6,9 +6,10 @@
 from jax.sharding import PartitionSpec as P
 
 MESH = pl.DeviceIdType.MESH
-PIECES = (7, 7)
+PIECES = (6, 4, 4)
 N = len(PIECES)
 LAST = N - 1
+EDGE = (2,)
 ZS = 12
 LAG = 2
 
@@ -24,7 +25,7 @@
 
 
 def hops(d, k, i):
-    return k < 3 or (k == 3 and (i % 2 == 0) == (d == 0))
+    return k < 3 or (k == 3 and (i == 0) == (d == 0))
 
 
 def count(d, i):
@@ -33,13 +34,14 @@
 
 def kernel(vol, w, out, *scratch):
     a_bufs, b_bufs = scratch[:N], scratch[N : 2 * N]
-    (halo, shifted, acc, own, swap_send, ring_send, ring_recv, z_send, z_recv,
+    (halo, shifted, acc, own, swap_send, ring_send, ring_recv, z_send, z_recv, edge_send,
      chip_send, chip_recv, halo_send, halo_recv, mid_sem, near_sem, far_sem, late_sem) = scratch[2 * N :]
     bufs = (a_bufs, b_bufs)
     s, ch = lax.axis_index("slab"), lax.axis_index("chan")
     y, xh = s // 2, s % 2
     core, xl, z = ch % 2, (ch // 2) % 2, ch // 4
     half = z % 2
+    at_edge = (z == 0) | (z == ZS - 1)
     is_late = (s == 0) & (ch == 0)
     is_host = (s == 0) & (ch == 1)
     meets_late = (s == 1) & (ch == 0)
@@ -173,6 +175,21 @@
             ref if src is None else src, ref,
             ring_send.at[kind, d, i], ring_recv.at[kind, d, k, i], ring_of(kind)[d],
         )
+
+    def edge_copy(d, k, i, kind, src=None):
+        ref = b_bufs[i].at[block_of(d, k - 1), kind]
+        return remote(
+            ref if src is None else src, ref,
+            edge_send.at[kind, d, i], z_recv.at[kind, d, k, i], ring_of(kind)[d],
+        )
+
+    def edge_events(k, i, kind):
+        @pl.when(at_edge)
+        def _():
+            for d in (0, 1):
+                land(z_recv.at[kind, d, k, i], b_bufs[i].at[block_of(d, k), kind])
+                if hops(d, k + 1, i):
+                    edge_copy(d, k + 1, i, kind).start()
 
     def z_copy(d, k, i, to, kind):
         block = block_of(d, k)
@@ -211,6 +228,12 @@
         for i in range(N):
             src, mine = own_src(1, i), b_bufs[i].at[y, kind]
             remote(src, mine, swap_send.at[kind, 1, i], own.at[kind, 1, i], swap_of(kind)).start()
+            if i in EDGE:
+
+                @pl.when(at_edge)
+                def _():
+                    for d in (0, 1):
+                        edge_copy(d, 0, i, kind, src).start()
 
     def keep(kind):
         for which in (0, 1):
@@ -227,19 +250,30 @@
                 ring_copy(d, k + 1, i, kind).start()
             away = (z == 1) if d == 0 else (z == ZS - 2)
 
-            @pl.when(has_z[d])
+            toward = (z == ZS - 2) if d == 0 else (z == 1)
+
+            @pl.when(has_z[d] & jnp.logical_not(toward) if i in EDGE else has_z[d])
             def _():
                 z_copy(d, k, i, d, kind).start()
 
-            @pl.when(away)
-            def _():
-                z_copy(d, k, i, 1 - d, kind).start()
+            if i not in EDGE:
+
+                @pl.when(away)
+                def _():
+                    z_copy(d, k, i, 1 - d, kind).start()
 
     def z_events(k, i, kind):
         for d in (0, 1):
             if not hops(d, k, i):
                 continue
-            land(z_recv.at[kind, d, k, i], b_bufs[i].at[block_of(d, k), kind])
+            if i in EDGE and k < 3:
+
+                @pl.when(jnp.logical_not(at_edge))
+                def _():
+                    land(z_recv.at[kind, d, k, i], b_bufs[i].at[block_of(d, k), kind])
+
+            else:
+                land(z_recv.at[kind, d, k, i], b_bufs[i].at[block_of(d, k), kind])
 
     depth_copies = [
         remote(vol.at[1:2], halo.at[0:1, 1:3], halo_send.at[0], halo_recv.at[0], depth_dev[0]),
@@ -249,6 +283,13 @@
         remote(halo.at[:, 2:3], halo.at[:, 0:1], halo_send.at[2], halo_recv.at[2], row_dev[0]),
         remote(halo.at[:, 1:2], halo.at[:, 3:4], halo_send.at[3], halo_recv.at[3], row_dev[1]),
     ]
+
+    late_row = remote(
+        halo.at[1:3, 2:3], halo.at[1:3, 0:1], halo_send.at[2], halo_recv.at[2], row_dev[0]
+    )
+    corner = remote(
+        vol.at[0:1, 1:2], halo.at[3:4, 0:1], halo_send.at[4], halo_recv.at[4], (0, 1)
+    )
 
     def halo_rows():
         for d in (0, 1):
@@ -321,7 +362,8 @@
     @pl.when(is_late)
     def _():
         depth_copies[0].start()
-        halo_rows()
+        land(mid_sem, halo.at[1:3, 1:3])
+        late_row.start()
 
     @pl.when(active)
     def _():
@@ -354,10 +396,14 @@
         for k in range(4):
             for i in range(N):
                 ring_events(k, i, core)
+                if k > 0 and i in EDGE:
+                    edge_events(k - 1, i, core)
 
                 @pl.when(is_host)
                 def _():
                     ring_events(k, i, 0)
+                    if k > 0 and i in EDGE:
+                        edge_events(k - 1, i, 0)
 
                 if k == 3:
 
@@ -376,6 +422,10 @@
                     def _():
                         depth_copies[d].start()
 
+                @pl.when(meets_late)
+                def _():
+                    corner.start()
+
                 @pl.when(here)
                 def _():
                     for which in (0, 1):
@@ -386,6 +436,12 @@
                 def _():
                     for i in range(N):
                         land(own.at[core, 1, i], b_bufs[i].at[y, core])
+                        if i in EDGE:
+
+                            @pl.when(at_edge)
+                            def _():
+                                for d in (0, 1):
+                                    edge_copy(d, 0, i, core).start()
 
             if k == 2:
 
@@ -394,9 +450,7 @@
                     pl.semaphore_wait(late_sem, 1)
                     depth_copies[1].start()
 
-                @pl.when(jnp.logical_not(meets_late))
-                def _():
-                    halo_rows()
+                halo_rows()
 
                 @pl.when(is_host)
                 def _():
@@ -408,10 +462,6 @@
                     for i in range(N):
                         host_give(0, i, True)
 
-        @pl.when(meets_late)
-        def _():
-            halo_rows()
-
         @pl.when(is_host)
         def _():
             for i in range(N):
@@ -430,9 +480,18 @@
 
     for d in (0, 1):
 
-        @pl.when(has_row[1 - d])
+        @pl.when(has_row[1 - d] & jnp.logical_not(is_host) if d == 0 else has_row[1 - d])
         def _():
             row_copies[d].wait_recv()
+
+    @pl.when(is_host)
+    def _():
+        late_row.wait_recv()
+        corner.wait_recv()
+
+    @pl.when(is_late)
+    def _():
+        depth_copies[1].wait_recv()
 
     for d in range(4):
         spread(d)
@@ -468,9 +527,17 @@
                 def _():
                     left(b_bufs[i], count(d, i), z_send.at[kind, d, i])
 
-                @pl.when(toward)
-                def _():
-                    left(b_bufs[i], both, z_send.at[kind, d, i])
+                if i in EDGE:
+
+                    @pl.when(at_edge)
+                    def _():
+                        left(b_bufs[i], count(d, i), edge_send.at[kind, d, i])
+
+                else:
+
+                    @pl.when(toward)
+                    def _():
+                        left(b_bufs[i], both, z_send.at[kind, d, i])
 
     def gone_own(kind):
         for which in (0, 1):
@@ -505,9 +572,17 @@
         def _():
             depth_copies[d].wait_send()
 
-        @pl.when(has_row[d])
+        @pl.when(has_row[d] & active if d == 0 else has_row[d])
         def _():
             row_copies[d].wait_send()
+
+    @pl.when(is_late)
+    def _():
+        late_row.wait_send()
+
+    @pl.when(meets_late)
+    def _():
+        corner.wait_send()
 
 
 def solution(mesh):
@@ -530,10 +605,11 @@
                 dma((2, 2, 4, N)),
                 dma((2, 2, N)),
                 dma((2, 2, 4, N)),
+                dma((2, 2, N)),
                 dma((2, N)),
                 dma((2, N)),
-                dma((4,)),
-                dma((4,)),
+                dma((5,)),
+                dma((5,)),
                 dma(()),
                 regular,
                 regular,

time: 34.6 us -> 32.8 us (0.948)
  the two profiles are of different devices: /device:TPU:1 before, /device:TPU:134 now
where the time goes in v4:
time: 32.8 us; the launch traced here: 32.7 us
  Pallas kernels  32 us (98%)
  local copies, waits for them, and re-layouts  0.66 us (2%)
    pallas_call x1, Pallas kernels, local(): pl.pallas_call(kernel, out_shape=pltpu.VMEM(volume.shape, jnp.bfloat16),...  32 us
    unnamed x1, local copies, waits for them, and re-layouts  0.66 us

profile of v4, /device:TPU:134, one launch (start us, length us, event | category | flops | bytes accessed | tf_op | source)
XLA Modules:
  0.0 32.7 jit_solution(195041708196118627)
XLA Ops:
  0.0 32.0 %conv_gather.1 = bf16[2,2,64,256]{3,2,1,0:T(8,128)(2,1)S(1)} custom-call(bf16[2,2,64,256]{3,2,1,0:T(8,128)(2,1)} %vol.1, bf16[16,6912]{1,0:T(8,128)(2,1)} %bitcast.1), custom_call_target="tpu_custom_call" | custom-call | tf_op jit(solution)/shard_map/conv_gather/pallas_call | solution.py:591
  32.0 0.7 %copy.4 = bf16[2,2,64,256]{3,2,1,0:T(8,128)(2,1)} copy(bf16[2,2,64,256]{3,2,1,0:T(8,128)(2,1)S(1)} %conv_gather.1) | data formatting | bytes 262144

commit v5 on v4

--- a/solution.py
+++ b/solution.py
@@ -85,6 +85,21 @@
     def across_of(kind):
         return (own_devices if kind is core else zero_devices)[3]
 
+    def slot(kind):
+        return 0 if kind is core else 1
+
+    def guest(dev):
+        return ((core == 0) & (dev[0] == 0) & (dev[1] == 1)).astype(jnp.int32)
+
+    ring_guest = [guest(own_devices[0][d]) for d in (0, 1)]
+    z_guest = guest(own_devices[2][1])
+
+    def ring_slot(d, kind):
+        return ring_guest[d] if kind is core else 0
+
+    def z_slot(to, kind):
+        return z_guest if kind is core and to == 1 else 0
+
     partner = (s, ch + 1 - 2 * core)
     has_z = (z < ZS - 1, z > 0)
     depth_dev = ((jnp.minimum(s + 1, 15), ch), (jnp.maximum(s - 1, 0), ch))
@@ -173,21 +188,21 @@
         ref = a_bufs[i].at[block_of(d, k - 1), kind]
         return remote(
             ref if src is None else src, ref,
-            ring_send.at[kind, d, i], ring_recv.at[kind, d, k, i], ring_of(kind)[d],
+            ring_send.at[slot(kind), d, i], ring_recv.at[ring_slot(d, kind), d, k, i], ring_of(kind)[d],
         )
 
     def edge_copy(d, k, i, kind, src=None):
         ref = b_bufs[i].at[block_of(d, k - 1), kind]
         return remote(
             ref if src is None else src, ref,
-            edge_send.at[kind, d, i], z_recv.at[kind, d, k, i], ring_of(kind)[d],
+            edge_send.at[slot(kind), d, i], z_recv.at[ring_slot(d, kind), d, k, i], ring_of(kind)[d],
         )
 
     def edge_events(k, i, kind):
         @pl.when(at_edge)
         def _():
             for d in (0, 1):
-                land(z_recv.at[kind, d, k, i], b_bufs[i].at[block_of(d, k), kind])
+                land(z_recv.at[slot(kind), d, k, i], b_bufs[i].at[block_of(d, k), kind])
                 if hops(d, k + 1, i):
                     edge_copy(d, k + 1, i, kind).start()
 
@@ -199,7 +214,7 @@
             src = a_bufs[i].at[block, kind]
         return remote(
             src, b_bufs[i].at[block, kind],
-            z_send.at[kind, to, i], z_recv.at[kind, d, k, i], z_of(kind)[to],
+            z_send.at[slot(kind), to, i], z_recv.at[z_slot(to, kind), d, k, i], z_of(kind)[to],
         )
 
     def chip_give(which, i):
@@ -220,14 +235,14 @@
     def give_a(kind):
         for i in range(N):
             src, mine = own_src(0, i), a_bufs[i].at[y, kind]
-            remote(src, mine, swap_send.at[kind, 0, i], own.at[kind, 0, i], swap_of(kind)).start()
+            remote(src, mine, swap_send.at[slot(kind), 0, i], own.at[0, 0, i], swap_of(kind)).start()
             for d in (0, 1):
                 ring_copy(d, 0, i, kind, src).start()
 
     def give_b(kind):
         for i in range(N):
             src, mine = own_src(1, i), b_bufs[i].at[y, kind]
-            remote(src, mine, swap_send.at[kind, 1, i], own.at[kind, 1, i], swap_of(kind)).start()
+            remote(src, mine, swap_send.at[slot(kind), 1, i], own.at[0, 1, i], swap_of(kind)).start()
             if i in EDGE:
 
                 @pl.when(at_edge)
@@ -239,15 +254,18 @@
         for which in (0, 1):
             for i in range(N):
                 src, mine = own_src(which, i), bufs[which][i].at[y, kind]
-                pltpu.make_async_copy(src, mine, own.at[kind, which, i]).start()
+                pltpu.make_async_copy(src, mine, own.at[slot(kind), which, i]).start()
 
     def ring_events(k, i, kind):
         for d in (0, 1):
             if not hops(d, k, i):
                 continue
-            land(ring_recv.at[kind, d, k, i], a_bufs[i].at[block_of(d, k), kind])
+            land(ring_recv.at[slot(kind), d, k, i], a_bufs[i].at[block_of(d, k), kind])
             if hops(d, k + 1, i):
                 ring_copy(d, k + 1, i, kind).start()
+        for d in (0, 1):
+            if not hops(d, k, i):
+                continue
             away = (z == 1) if d == 0 else (z == ZS - 2)
 
             toward = (z == ZS - 2) if d == 0 else (z == 1)
@@ -270,10 +288,10 @@
 
                 @pl.when(jnp.logical_not(at_edge))
                 def _():
-                    land(z_recv.at[kind, d, k, i], b_bufs[i].at[block_of(d, k), kind])
+                    land(z_recv.at[slot(kind), d, k, i], b_bufs[i].at[block_of(d, k), kind])
 
             else:
-                land(z_recv.at[kind, d, k, i], b_bufs[i].at[block_of(d, k), kind])
+                land(z_recv.at[slot(kind), d, k, i], b_bufs[i].at[block_of(d, k), kind])
 
     depth_copies = [
         remote(vol.at[1:2], halo.at[0:1, 1:3], halo_send.at[0], halo_recv.at[0], depth_dev[0]),
@@ -387,7 +405,7 @@
         @pl.when(jnp.logical_not(here))
         def _():
             for i in range(N):
-                land(own.at[core, 0, i], a_bufs[i].at[y, core])
+                land(own.at[0, 0, i], a_bufs[i].at[y, core])
                 for d in (0, 1):
                     ring_copy(d, 0, i, core, a_bufs[i].at[y, core]).start()
 
@@ -430,12 +448,12 @@
                 def _():
                     for which in (0, 1):
                         for i in range(N):
-                            land(own.at[core, which, i], bufs[which][i].at[y, core])
+                            land(own.at[0, which, i], bufs[which][i].at[y, core])
 
                 @pl.when(jnp.logical_not(here))
                 def _():
                     for i in range(N):
-                        land(own.at[core, 1, i], b_bufs[i].at[y, core])
+                        land(own.at[0, 1, i], b_bufs[i].at[y, core])
                         if i in EDGE:
 
                             @pl.when(at_edge)
@@ -458,7 +476,7 @@
                     row_copies[1].start()
                     for which in (0, 1):
                         for i in range(N):
-                            land(own.at[0, which, i], bufs[which][i].at[y, 0])
+                            land(own.at[1, which, i], bufs[which][i].at[y, 0])
                     for i in range(N):
                         host_give(0, i, True)
 
@@ -520,29 +538,29 @@
         for i in range(N):
             both = count(0, i) + count(1, i)
             for d in (0, 1):
-                left(a_bufs[i], count(d, i), ring_send.at[kind, d, i])
+                left(a_bufs[i], count(d, i), ring_send.at[slot(kind), d, i])
                 toward = (z == ZS - 2) if d == 0 else (z == 1)
 
                 @pl.when(has_z[d] & jnp.logical_not(toward))
                 def _():
-                    left(b_bufs[i], count(d, i), z_send.at[kind, d, i])
+                    left(b_bufs[i], count(d, i), z_send.at[slot(kind), d, i])
 
                 if i in EDGE:
 
                     @pl.when(at_edge)
                     def _():
-                        left(b_bufs[i], count(d, i), edge_send.at[kind, d, i])
+                        left(b_bufs[i], count(d, i), edge_send.at[slot(kind), d, i])
 
                 else:
 
                     @pl.when(toward)
                     def _():
-                        left(b_bufs[i], both, z_send.at[kind, d, i])
+                        left(b_bufs[i], both, z_send.at[slot(kind), d, i])
 
     def gone_own(kind):
         for which in (0, 1):
             for i in range(N):
-                left(bufs[which][i], 1, swap_send.at[kind, which, i])
+                left(bufs[which][i], 1, swap_send.at[slot(kind), which, i])
 
     @pl.when(active)
     def _():

time: 32.8 us -> 32.8 us (level)
  no operation moved by 1% of the time
where the time goes in v5:
time: 32.8 us; the launch traced here: 32.7 us
  Pallas kernels  32 us (98%)
  local copies, waits for them, and re-layouts  0.66 us (2%)
    pallas_call x1, Pallas kernels, local(): pl.pallas_call(kernel, out_shape=pltpu.VMEM(volume.shape, jnp.bfloat16),...  32 us
    unnamed x1, local copies, waits for them, and re-layouts  0.66 us

profile of v5, /device:TPU:134, one launch (start us, length us, event | category | flops | bytes accessed | tf_op | source)
XLA Modules:
  0.0 32.7 jit_solution(13975810881400402840)
XLA Ops:
  0.0 32.0 %conv_gather.1 = bf16[2,2,64,256]{3,2,1,0:T(8,128)(2,1)S(1)} custom-call(bf16[2,2,64,256]{3,2,1,0:T(8,128)(2,1)} %vol.1, bf16[16,6912]{1,0:T(8,128)(2,1)} %bitcast.1), custom_call_target="tpu_custom_call" | custom-call | tf_op jit(solution)/shard_map/conv_gather/pallas_call | solution.py:609
  32.0 0.7 %copy.4 = bf16[2,2,64,256]{3,2,1,0:T(8,128)(2,1)} copy(bf16[2,2,64,256]{3,2,1,0:T(8,128)(2,1)S(1)} %conv_gather.1) | data formatting | bytes 262144
